TPU v7x, 256 devices: a whole 4x4x8 slice. The times are simulated.
256 devices in a mesh: layer: 2 (over core), ex: 128 (over z, y, x).
Axes of the slice: x: 4, y: 4, z: 8, core: 2. Of those that a mesh axis runs over, the one named last changes fastest.
Arguments:
- train_sketch: bfloat16 [12, 65536, 256], P('layer', 'ex')
- val_sketch: bfloat16 [12, 4096, 256], P('layer', 'ex')
- first_moment: float32 [12, 256], P('layer'), may hold values from -0.6 to 0.6
- second_moment: float32 [12, 256], P('layer'), may hold values from 0.01 to 1
- train_pair: int32 [65536], P('ex'), may hold values from 0 to 15
- val_pair: int32 [4096], P('ex'), may hold values from 0 to 15
- block_mask: int32 [16, 16], replicated, may hold values 0 or 1
Outputs:
- scores: bfloat16 [32768, 2, 4096], P('ex', 'layer')
All inputs are finite; a program needn't handle non-finite values.
Results may differ from a plain program's by a relative error of at most 0.0058.
Values may be sent and summed in bfloat16 or wider, within the bound.
No kernel may reach another device: no remote copies, remote signals or barrier semaphores. Data moves between devices by JAX's collectives and lax.ppermute only.
A program may use at most 128 MiB of HBM per device.

v0:
```python
import jax
import jax.numpy as jnp
from jax import lax
from jax.sharding import PartitionSpec as P


def precondition(grad, first_moment, second_moment):
    return (0.9 * first_moment[:, None, :] + 0.1 * grad) / (
        jnp.sqrt(0.999 * second_moment[:, None, :] + 0.001 * grad * grad) + 1e-08
    )


def squares(values):
    return jnp.sum(values * values, axis=(0, 2))


def unit_rows(values, total_sq, scale_factor):
    return (values * (scale_factor * lax.rsqrt(total_sq + 1e-06))[None, :, None]).astype(
        jnp.bfloat16
    )


def contract(left, right):
    return lax.dot_general(
        left, right, (((0, 2), (0, 2)), ((), ())), preferred_element_type=jnp.float32
    )


def local(train_sketch, val_sketch, first_moment, second_moment, train_pair, val_pair, block_mask):
    lay_dev, tr_ex, width = train_sketch.shape
    layer_count = lax.axis_size("layer")
    rows_here = tr_ex // layer_count
    scale_factor = float(lay_dev * layer_count * width) ** 0.25
    pair_count = block_mask.shape[0]
    labels = jnp.arange(pair_count, dtype=jnp.int32)
    val_all = lax.all_gather(val_sketch, "ex", axis=1, tiled=True)
    val_labels = lax.all_gather(val_pair, "ex", axis=0, tiled=True)
    val_onehot = (labels[:, None] == val_labels[None, :]).astype(jnp.bfloat16)
    pairs_here = lax.dynamic_slice_in_dim(
        train_pair, lax.axis_index("layer") * rows_here, rows_here, 0
    )
    mine = lax.all_to_all(train_sketch, "layer", split_axis=1, concat_axis=0, tiled=True)
    first_all, second_all = (
        lax.all_gather(first_moment, "layer", axis=0, tiled=True),
        lax.all_gather(second_moment, "layer", axis=0, tiled=True),
    )
    val_full = lax.all_gather(val_all, "layer", axis=0, tiled=True)
    pre = precondition(mine.astype(jnp.float32), first_all, second_all)
    unit_train = unit_rows(pre, squares(pre), scale_factor)
    val_float = val_full.astype(jnp.float32)
    unit_val = unit_rows(val_float, squares(val_float), scale_factor)
    raw = contract(unit_train, unit_val)
    train_onehot = (pairs_here[:, None] == labels[None, :]).astype(jnp.bfloat16)
    row_mask = jnp.dot(
        train_onehot, block_mask.astype(jnp.bfloat16), preferred_element_type=jnp.float32
    ).astype(jnp.bfloat16)
    weights = jnp.dot(row_mask, val_onehot, preferred_element_type=jnp.float32)
    return (raw * weights).astype(jnp.bfloat16)[:, None, :]


def solution(mesh):
    placed = (
        P("layer", "ex", None),
        P("layer", "ex", None),
        P("layer", None),
        P("layer", None),
        P("ex"),
        P("ex"),
        P(),
    )
    return jax.shard_map(
        local, mesh=mesh, in_specs=placed, out_specs=P("ex", "layer", None), check_vma=False
    )
```

profile of v0, /device:TPU:0, one launch (start us, length us, event | category | flops | bytes accessed | tf_op | source)
XLA Modules:
  0.0 894.7 jit_solution(7352749476020731532)
XLA Ops:
  6.5 0.0 all-gather.5.cloned.1.call-start
  6.5 0.7 all-gather.5.cloned.1.call-update
  7.3 0.0 all-gather.7.cloned.1.call-start
  7.3 143.9 %all-gather.5.cloned.1.call-done = bf16[6,4096,256]{2,1,0:T(8,128)(2,1)} async-done(((bf16[6,32,256]{2,1,0:T(8,128)(2,1)}), bf16[6,4096,256]{2,1,0:T(8,128)(2,1)}) %all-gather.5.cloned.1.call-update) | async-done | bytes 12582928 | tf_op jit(solution)/shard_map/all_gather | solution.py:36
  151.2 0.0 copy-start
  151.2 0.0 all-gather.7.cloned.1.call-update
  151.2 1.4 copy-done
  152.6 0.0 copy-start.2
  152.6 0.0 copy-start.3
  152.6 2.2 copy.14
  154.9 3.8 all-to-all-start
  158.6 0.0 copy-done.2
  158.6 2.6 all-gather
  161.3 0.0 copy-done.3
  161.3 1.8 all-gather.1
  163.1 0.0 all-to-all-done
  163.1 0.3 convert_bitcast_fusion
  163.5 0.0 copy-start.6
  163.5 0.0 copy-start.4
  163.5 0.0 copy-start.5
  163.5 3.4 copy.15
  166.9 0.0 copy-done.6
  166.9 0.6 dynamic-slice
  168.1 0.0 copy-done.4
  168.1 0.1 dynamic_slice.3
  168.2 0.0 copy-done.5
  168.2 0.2 dynamic-update-slice
  168.5 684.9 %all-reduce = s32[4096]{0:T(1024)S(1)} all-reduce(s32[4096]{0:T(1024)S(1)} %dynamic-update-slice), channel_id=1, replica_groups=mesh['layer'=2,'ex'=128] {'ex'}, use_global_device_ids=true, to_apply=%add | all-reduce | flops 4096 | bytes 32768
  853.4 2.9 fusion.15
  856.3 3.6 fusion.22
  859.9 0.0 all-gather.7.cloned.1.call-done
  859.9 10.3 %fusion = f32[4096]{0:T(1024)S(1)} fusion(bf16[12,4096,256]{2,1,0:T(8,128)(2,1)} %all-gather.7.cloned.1.call-done), kind=kLoop, calls=%fused_computation.2 | loop fusion | flops 37744640 | bytes 25182208 | tf_op jit(solution)/shard_map/reduce_sum | solution.py:14
  870.3 0.0 copy-start.1
  870.3 13.1 %fusion.5 = f32[256,4096]{1,0:T(8,128)} fusion(bf16[12,256,256]{2,1,0:T(8,128)(2,1)S(1)} %fusion.22, bf16[12,4096,256]{2,1,0:T(8,128)(2,1)} %all-gather.7.cloned.1.call-done, f32[4096]{0:T(1024)S(1)} %rsqrt_multiply_fusion), kind=kOutput, calls=%fused_computation.7 | convolution fusion | flops 6480199680 | bytes 30949376 | tf_op jit(solution)/shard_map/dot_general | solution.py:24
  883.4 0.0 copy-done.1
  883.4 4.5 fusion.9
  (7 shorter events, 0.0 us)
Async XLA Ops:
  6.5 144.7 %all-gather.5.cloned.1.call-start = ((), (), s32[]{:S(2)}) async-start(), calls=%async_computation.1 | async-start | bytes 12681216 | tf_op jit(solution)/shard_map/all_gather | solution.py:36
  7.3 852.7 %all-gather.7.cloned.1.call-start = ((), (), s32[]{:S(2)}) async-start(), calls=%async_computation.2 | async-start | bytes 37748736 | tf_op jit(solution)/shard_map/all_gather | solution.py:47
  151.2 1.4 copy-start
  152.6 6.0 copy-start.2
  152.6 8.7 copy-start.3
  154.9 8.3 all-to-all-start
  163.5 3.4 copy-start.6
  163.5 4.7 copy-start.4
  163.5 4.7 copy-start.5
  870.3 13.1 %copy-start.1 = (s32[16,16]{1,0:T(8,128)S(1)}, s32[16,16]{1,0:T(8,128)}, u32[]{:S(2)}) copy-start(s32[16,16]{1,0:T(8,128)} %param.13) | copy-start | bytes 3076
Sparse Core Ops, SparseCore 0:
  10.9 140.2 all-gather.4
  153.0 42.9 all-gather.6
where the time goes:
time: 895 us
  blocking collectives  689 us (77%)
  waiting for transfers between devices  145 us (16%)
  matrix products  17.6 us (2%)
  other arithmetic  17.2 us (2%)
  between operations  14.2 us (2%)
    unnamed x1, blocking collectives  685 us
    all_gather x1, waiting for transfers between devices, local(): val_all = lax.all_gather(val_sketch, 'ex', axis=1, tiled=True)  144 us
  transfers between devices with their start and end apart: 3, of which 1 were waited for; matrix products, arithmetic and copies ran while one was open for 1% of the time, Pallas kernels for 0%

commit v1 on v0

--- a/solution.py
+++ b/solution.py
@@ -2,6 +2,13 @@
 import jax.numpy as jnp
 from jax import lax
 from jax.sharding import PartitionSpec as P
+
+
+def swapped_in(x, axis, dim):
+    size = lax.axis_size(axis)
+    parts = jnp.stack([x for _ in range(size)])
+    parts = lax.all_to_all(parts, axis, split_axis=0, concat_axis=0)
+    return jnp.concatenate(parts, axis=dim)
 
 
 def precondition(grad, first_moment, second_moment):
@@ -33,7 +40,7 @@
     scale_factor = float(lay_dev * layer_count * width) ** 0.25
     pair_count = block_mask.shape[0]
     labels = jnp.arange(pair_count, dtype=jnp.int32)
-    val_all = lax.all_gather(val_sketch, "ex", axis=1, tiled=True)
+    val_all = swapped_in(val_sketch, "ex", 1)
     val_labels = lax.all_gather(val_pair, "ex", axis=0, tiled=True)
     val_onehot = (labels[:, None] == val_labels[None, :]).astype(jnp.bfloat16)
     pairs_here = lax.dynamic_slice_in_dim(

time: 895 us -> 1050 us (1.17)
  blocking collectives: 689 us -> 979 us
  waiting for transfers between devices: 145 us -> 2.88 us
  local copies, waits for them, and re-layouts: 7.94 us -> 20.2 us
    all_to_all x0 -> x1, blocking collectives: none -> 290 us  [swapped_in(): parts = lax.all_to_all(parts, axis, split_axis=0, concat_axis=0)]
    all_gather x1 -> x0, waiting for transfers between devices: 144 us -> none  [local(): val_all = lax.all_gather(val_sketch, 'ex', axis=1, tiled=True)]
  transfers between devices with their start and end apart: 3 -> 2, of which waited for: 1 -> 1; matrix products, arithmetic and copies ran while one was open for 1% -> 1% of each run, Pallas kernels for 0% -> 0%
where the time goes in v1:
time: 1050 us
  blocking collectives  979 us (93%)
  local copies, waits for them, and re-layouts  20.2 us (2%)
  matrix products  17.5 us (2%)
  other arithmetic  17.2 us (2%)
  between operations  14.2 us (1%)
    unnamed x1, blocking collectives  685 us
    all_to_all x1, blocking collectives, swapped_in(): parts = lax.all_to_all(parts, axis, split_axis=0, concat_axis=0)  290 us
  transfers between devices with their start and end apart: 2, of which 1 were waited for; matrix products, arithmetic and copies ran while one was open for 1% of the time, Pallas kernels for 0%

profile of v1, /device:TPU:0, one launch (start us, length us, event | category | flops | bytes accessed | tf_op | source)
XLA Modules:
  0.0 1054.5 jit_solution(16616266552468745484)
XLA Ops:
  6.5 0.0 all-gather.4.cloned.1.call-start
  6.5 7.0 stack.2
  13.6 289.9 %all_to_all.14 = bf16[128,6,32,256]{3,2,1,0:T(8,128)(2,1)S(1)} all-to-all(bf16[128,6,32,256]{3,2,1,0:T(8,128)(2,1)} %stack.2), channel_id=1, replica_groups=mesh['layer'=2,'ex'=128] {'ex'}, dimensions={0} | all-to-all | bytes 25165824 | tf_op jit(solution)/shard_map/all_to_all | solution.py:10
  303.5 5.2 copy.18
  308.7 0.0 copy-start
  308.7 0.0 all-gather.4.cloned.1.call-update
  308.8 1.4 copy-done
  310.1 2.2 copy.16
  312.4 3.8 all-to-all-start
  316.2 2.8 all-to-all-done
  319.0 0.3 convert_bitcast_fusion
  319.3 0.0 copy-start.2
  319.4 0.0 copy-start.3
  319.4 0.0 copy-start.6
  319.4 0.0 copy-start.4
  319.4 0.0 copy-start.5
  319.4 3.3 copy.17
  322.7 0.0 copy-done.2
  322.7 1.8 all-gather.1
  324.5 0.0 copy-done.3
  324.5 1.8 all-gather
  326.3 0.0 copy-done.6
  326.4 0.6 dynamic-slice
  327.6 0.0 copy-done.4
  327.6 0.1 dynamic_slice.3
  327.7 0.0 copy-done.5
  327.7 0.2 dynamic-update-slice
  327.9 685.4 %all-reduce = s32[4096]{0:T(1024)S(1)} all-reduce(s32[4096]{0:T(1024)S(1)} %dynamic-update-slice), channel_id=1, replica_groups=mesh['layer'=2,'ex'=128] {'ex'}, use_global_device_ids=true, to_apply=%add | all-reduce | flops 4096 | bytes 32768
  1013.3 2.9 fusion.15
  1016.2 3.6 fusion.22
  1019.8 0.0 all-gather.4.cloned.1.call-done
  1019.8 10.3 fusion
  1030.2 0.0 copy-start.1
  1030.2 13.0 %fusion.5 = f32[256,4096]{1,0:T(8,128)} fusion(bf16[12,256,256]{2,1,0:T(8,128)(2,1)S(1)} %fusion.22, bf16[12,4096,256]{2,1,0:T(8,128)(2,1)} %all-gather.4.cloned.1.call-done, f32[4096]{0:T(1024)S(1)} %rsqrt_multiply_fusion), kind=kOutput, calls=%fused_computation.7 | convolution fusion | flops 6480199680 | bytes 30949376 | tf_op jit(solution)/shard_map/dot_general | solution.py:31
  1043.2 0.0 copy-done.1
  1043.2 4.5 fusion.9
  (7 shorter events, 0.0 us)
Async XLA Ops:
  6.5 1013.3 %all-gather.4.cloned.1.call-start = ((), (), s32[]{:S(2)}) async-start(), calls=%async_computation.2 | async-start | bytes 37748736 | tf_op jit(solution)/shard_map/all_gather | solution.py:54
  308.7 1.4 copy-start
  312.4 6.6 all-to-all-start
  319.3 3.4 copy-start.2
  319.4 5.2 copy-start.3
  319.4 7.0 copy-start.6
  319.4 8.2 copy-start.4
  319.4 8.3 copy-start.5
  1030.2 13.0 %copy-start.1 = (s32[16,16]{1,0:T(8,128)S(1)}, s32[16,16]{1,0:T(8,128)}, u32[]{:S(2)}) copy-start(s32[16,16]{1,0:T(8,128)} %param.13) | copy-start | bytes 3076
Sparse Core Ops, SparseCore 0:
  308.9 41.6 all-gather.3
